TPU v7x, 32 devices: a whole 2x2x4 slice. The times are simulated.
32 devices in a mesh: box: 2 (over y), gx: 8 (over z, x), gy: 2 (over core).
Axes of the slice: x: 2, y: 2, z: 4, core: 2. Of those that a mesh axis runs over, the one named last changes fastest.
Arguments:
- positions: float32 [16, 4, 3, 256], P(('box', 'gx'), 'gy'), parts along dimension 0, may hold values from 0 to 18, as said below
- polarizability: float32 [16, 4, 256], P(('box', 'gx'), 'gy'), parts along dimension 0, may hold values from 0.3 to 1.5
- tile_counts: int32 [16, 4, 2], P(('box', 'gx'), 'gy'), parts along dimension 0, may hold values from 80 to 128, as said below
- molecules: int32 [16, 4, 256], P(('box', 'gx'), 'gy'), parts along dimension 0, may hold values from 0 to 170, as said below
- perm_field: float32 [16, 4, 3, 256], P(('box', 'gx'), 'gy'), parts along dimension 0, may hold values from -6 to 6
- dipoles: float32 [16, 4, 3, 256], P(('box', 'gx'), 'gy'), parts along dimension 0, may hold values from -4 to 4
- past_out: float32 [16, 4, 7, 3, 256], P(('box', 'gx'), 'gy'), parts along dimension 0, may hold values from -4 to 4
- past_res: float32 [16, 4, 7, 3, 256], P(('box', 'gx'), 'gy'), parts along dimension 0, may hold values from -15 to 15
Outputs:
- dipoles_next: float32 [16, 4, 3, 256], P(('box', 'gx'), 'gy'), parts along dimension 0
- diis_weights: float32 [16], P('box'), parts along dimension 0
There are 2 independent parts, one for each index of `box`. A program takes and returns all parts, laid end to end along the dimension named above; each array names one. Nothing has to cross between parts.
Inputs may be any that keep to these rules, and one draw needn't show every extreme that they name: x and y in [0, 9); z of an atom in z-tile t lies in [9 t, 9 t + 9); padded slots carry positions too. `tile_counts`: some z-tile is full. `molecules`: a group holds at most three atoms, all of one z-tile of one cell.
All inputs are finite; a program needn't handle non-finite values.
Results may differ from a plain program's by a relative error of at most 0.0003.
Values sent between devices are 32-bit elements; how exact they have to be, the bound alone decides.
A program may use at most 64 MiB of HBM per device.

v0:
```python
import jax
import jax.numpy as jnp
from jax import lax
from jax.sharding import PartitionSpec as P

ITERS = 2
CELL_SIDE = 9.0
CUTOFF_SQ = 81.0
SOFTENING = 0.25
THOLE_DAMP = 0.39
FAR_LIFT = 1000.0
NEIGHBOUR_X = (1.0, 0.0, 1.0, 1.0)
NEIGHBOUR_Y = (0.0, 1.0, 1.0, -1.0)


def from_behind(block, axis, distance):
    devices = range(lax.axis_size(axis))
    route = [((i - distance) % len(devices), i) for i in devices]
    return lax.ppermute(block, axis, route)


def pair_terms(
    target_coords,
    target_polar,
    target_groups,
    target_occupied,
    source_coords,
    source_polar,
    source_groups,
    source_occupied,
):
    displace = source_coords[:, None, :] - target_coords[:, :, None]
    square_dist = jnp.sum(displace * displace, axis=0) + SOFTENING
    distance = jnp.sqrt(square_dist)
    cube_dist = square_dist * distance
    damped = THOLE_DAMP * cube_dist / jnp.sqrt(target_polar[:, None] * source_polar[None, :])
    damping = jnp.exp(-damped)
    tapering = jnp.square(jnp.maximum(1.0 - square_dist / CUTOFF_SQ, 0.0))
    keeper = (target_groups[:, None] != source_groups[None, :]).astype(jnp.float32)
    weight = tapering * keeper * target_occupied[:, None] * source_occupied[None, :]
    isotropic = weight * -jnp.expm1(-damped) / cube_dist
    tensorial = 3.0 * weight * (1.0 - (1.0 + damped) * damping) / (cube_dist * square_dist)
    return (displace, isotropic, tensorial)


def field_targets(displace, isotropic, tensorial, source_dipole):
    projected = jnp.sum(displace * source_dipole[:, None, :], axis=0)
    return jnp.sum(displace * (tensorial * projected)[None], axis=2) - jnp.sum(
        isotropic[None] * source_dipole[:, None, :], axis=2
    )


def field_sources(displace, isotropic, tensorial, target_dipole):
    projected = jnp.sum(displace * target_dipole[:, :, None], axis=0)
    return jnp.sum(displace * (tensorial * projected)[None], axis=1) - jnp.sum(
        isotropic[None] * target_dipole[:, :, None], axis=1
    )


def tiled(values, filler, tile_count):
    shaped = values.reshape(values.shape[:-1] + (tile_count, values.shape[-1] // tile_count))
    widths = [(0, 0)] * (shaped.ndim - 2) + [(1, 1), (0, 0)]
    return jnp.pad(shaped, widths, constant_values=filler)


def padded_coords(coords, tile_count):
    marker = tiled(jnp.zeros_like(coords), 1.0, tile_count)
    lifted = jnp.array([0.0, 0.0, FAR_LIFT], jnp.float32).reshape(3, 1, 1)
    return tiled(coords, 0.0, tile_count) + marker * lifted


def band_sources(padded, tile_at):
    coords, polarity, groups, occupied, dipole = padded

    def flat_vector(member):
        window_part = lax.dynamic_slice_in_dim(member, tile_at, 3, 2)
        return jnp.transpose(window_part, (1, 0, 2, 3)).reshape(3, -1)

    def flat_scalar(member):
        return lax.dynamic_slice_in_dim(member, tile_at, 3, 1).reshape(-1)

    return (
        flat_vector(coords),
        flat_scalar(polarity),
        flat_scalar(groups),
        flat_scalar(occupied),
        flat_vector(dipole),
    )


def target_tile(own_cell, first_slot, tile_width):
    coords, polarity, groups, occupied = own_cell
    return (
        lax.dynamic_slice_in_dim(coords, first_slot, tile_width, 1),
        lax.dynamic_slice_in_dim(polarity, first_slot, tile_width, 0),
        lax.dynamic_slice_in_dim(groups, first_slot, tile_width, 0),
        lax.dynamic_slice_in_dim(occupied, first_slot, tile_width, 0),
    )


def four_static(packed):
    east_cells = from_behind(packed, "gx", -1)
    next_own, next_east = from_behind((packed[0], east_cells[0]), "gy", -1)
    prior_east = from_behind(east_cells[-1], "gy", 1)
    north_cells = jnp.concatenate([packed[1:], next_own[None]], axis=0)
    north_east = jnp.concatenate([east_cells[1:], next_east[None]], axis=0)
    south_east = jnp.concatenate([prior_east[None], east_cells[:-1]], axis=0)
    return jnp.stack([east_cells, north_cells, north_east, south_east], axis=1)


def four_dipole(dipole):
    east_cells = from_behind(dipole, "gx", -1)
    next_own, next_east = from_behind((dipole[0], east_cells[0]), "gy", -1)
    prior_east = from_behind(east_cells[-1], "gy", 1)
    north_cells = jnp.concatenate([dipole[1:], next_own[None]], axis=0)
    north_east = jnp.concatenate([east_cells[1:], next_east[None]], axis=0)
    south_east = jnp.concatenate([prior_east[None], east_cells[:-1]], axis=0)
    return jnp.stack([east_cells, north_cells, north_east, south_east], axis=1)


def half_statics(coords, polarity, groups, occupied, tile_count):
    cell_count = coords.shape[0]
    packed = jnp.concatenate([coords, polarity[:, None], occupied[:, None]], axis=1)
    nearby = four_static(packed)
    lift_x = jnp.array(NEIGHBOUR_X, jnp.float32) * CELL_SIDE
    lift_y = jnp.array(NEIGHBOUR_Y, jnp.float32) * CELL_SIDE
    lifted = jnp.stack([lift_x, lift_y, jnp.zeros_like(lift_x)], axis=1)
    nearby_coords = nearby[:, :, 0:3] + lifted[None, :, :, None]
    nearby_groups = jnp.full((cell_count, 4, coords.shape[-1]), -1, jnp.int32)
    own_padded = (
        padded_coords(coords[:, None], tile_count),
        tiled(polarity[:, None], 1.0, tile_count),
        tiled(groups[:, None], -1, tile_count),
        tiled(occupied[:, None], 0.0, tile_count),
    )
    nearby_padded = (
        padded_coords(nearby_coords, tile_count),
        tiled(nearby[:, :, 3], 1.0, tile_count),
        tiled(nearby_groups, -1, tile_count),
        tiled(nearby[:, :, 4], 0.0, tile_count),
    )
    return (own_padded, nearby_padded)


def half_cell(own_cell, own_band, nearby_band, dipole, tile_count):
    tile_width = dipole.shape[-1] // tile_count

    def one_tile(tile_at, carry):
        own_field, back_field = carry
        first_slot = tile_at * tile_width
        target = target_tile(own_cell, first_slot, tile_width)
        target_dipole = lax.dynamic_slice_in_dim(dipole, first_slot, tile_width, 1)
        source = band_sources(own_band, tile_at)
        displace, isotropic, tensorial = pair_terms(
            target[0], target[1], target[2], target[3], source[0], source[1], source[2], source[3]
        )
        inside = field_targets(displace, isotropic, tensorial, source[4])
        source = band_sources(nearby_band, tile_at)
        displace, isotropic, tensorial = pair_terms(
            target[0], target[1], target[2], target[3], source[0], source[1], source[2], source[3]
        )
        outside = field_targets(displace, isotropic, tensorial, source[4])
        returned = field_sources(displace, isotropic, tensorial, target_dipole)
        returned = jnp.transpose(returned.reshape(3, 4, 3, tile_width), (1, 0, 2, 3))
        own_field = lax.dynamic_update_slice_in_dim(own_field, inside + outside, first_slot, 1)
        window = lax.dynamic_slice_in_dim(back_field, tile_at, 3, 2) + returned
        back_field = lax.dynamic_update_slice_in_dim(back_field, window, tile_at, 2)
        return (own_field, back_field)

    initial = (
        jnp.zeros(dipole.shape, jnp.float32),
        jnp.zeros((4, 3, tile_count + 2, tile_width), jnp.float32),
    )
    own_field, back_field = lax.fori_loop(0, tile_count, one_tile, initial)
    return (own_field, back_field[:, :, 1:-1].reshape(4, 3, -1))


def half_field(own_cells, statics, dipole, tile_count):
    own_padded, nearby_padded = statics
    own_band = own_padded + (tiled(dipole[:, None], 0.0, tile_count),)
    nearby_band = nearby_padded + (tiled(four_dipole(dipole), 0.0, tile_count),)

    def per_cell(members):
        return half_cell(members[0], members[1], members[2], members[3], tile_count)

    own_field, back_field = lax.map(per_cell, (own_cells, own_band, nearby_band, dipole))
    north_part = back_field[:, 1]
    north_east = back_field[:, 2]
    south_east = back_field[:, 3]
    from_below, below_east = from_behind((north_part[-1], north_east[-1]), "gy", 1)
    from_above = from_behind(south_east[0], "gy", -1)
    from_south = jnp.concatenate([from_below[None], north_part[:-1]], axis=0)
    from_south_west = jnp.concatenate([below_east[None], north_east[:-1]], axis=0)
    from_north = jnp.concatenate([south_east[1:], from_above[None]], axis=0)
    eastward = back_field[:, 0] + from_south_west + from_north
    from_west = from_behind(eastward, "gx", 1)
    return own_field + from_south + from_west


def diis_weights(gram_matrix):
    lower = jnp.linalg.cholesky(gram_matrix)
    history = gram_matrix.shape[0]
    forward = []
    for row_at in range(history):
        running = jnp.ones((), gram_matrix.dtype)
        for col_at in range(row_at):
            running = running - lower[row_at, col_at] * forward[col_at]
        forward.append(running / lower[row_at, row_at])
    backward = [None] * history
    for row_at in reversed(range(history)):
        running = forward[row_at]
        for col_at in range(row_at + 1, history):
            running = running - lower[col_at, row_at] * backward[col_at]
        backward[row_at] = running / lower[row_at, row_at]
    solved = jnp.stack(backward)
    return solved / jnp.sum(solved)


def body(
    positions, polarizability, tile_counts, molecules, perm_field, dipoles, past_out, past_res
):
    counts = tile_counts[0]
    cell_count = counts.shape[0]
    tile_count = counts.shape[1]
    coords = positions[0]
    atom_slots = coords.shape[-1]
    tile_width = atom_slots // tile_count
    slot_index = lax.broadcasted_iota(jnp.int32, (cell_count, tile_count, tile_width), 2)
    occupied = (slot_index < counts[:, :, None]).astype(jnp.float32).reshape(cell_count, atom_slots)
    polarity = polarizability[0]
    groups = molecules[0]
    own_cells = (coords, polarity, groups, occupied)
    occupied_vec = occupied[:, None, :]
    scaled = occupied_vec * polarity[:, None, :]
    stored_out = jnp.moveaxis(past_out[0], 1, 0) * occupied_vec
    stored_res = jnp.moveaxis(past_res[0], 1, 0) * occupied_vec
    current = dipoles[0] * occupied_vec
    permanent = perm_field[0]
    statics = half_statics(coords, polarity, groups, occupied, tile_count)
    weights = jnp.zeros((stored_out.shape[0] + 1,), jnp.float32)
    for step_at in range(ITERS):
        induced = half_field(own_cells, statics, current, tile_count)
        jacobi = scaled * (permanent + induced)
        residual = jacobi - current
        outputs_all = jnp.concatenate([stored_out, jacobi[None]], 0)
        residual_all = jnp.concatenate([stored_res, residual[None]], 0)
        flattened = residual_all.reshape(residual_all.shape[0], -1)
        local_gram = jnp.dot(
            flattened,
            flattened.T,
            precision=lax.Precision.HIGHEST,
            preferred_element_type=jnp.float32,
        )
        gram_matrix = lax.psum(local_gram, ("gx", "gy"))
        weights = diis_weights(gram_matrix)
        current = jnp.sum(weights[:, None, None, None] * outputs_all, axis=0)
        stored_out = outputs_all[1:]
        stored_res = residual_all[1:]
    return (current[None], weights)


def solution(mesh):
    placed = (
        P(("box", "gx"), "gy", None, None),
        P(("box", "gx"), "gy", None),
        P(("box", "gx"), "gy", None),
        P(("box", "gx"), "gy", None),
        P(("box", "gx"), "gy", None, None),
        P(("box", "gx"), "gy", None, None),
        P(("box", "gx"), "gy", None, None, None),
        P(("box", "gx"), "gy", None, None, None),
    )
    return jax.shard_map(
        body,
        mesh=mesh,
        in_specs=placed,
        out_specs=(P(("box", "gx"), "gy", None, None), P("box")),
        check_vma=False,
    )
```

profile of v0, /device:TPU:0, one launch (start us, length us, event | category | flops | bytes accessed | tf_op | source)
XLA Modules:
  0.0 246.8 jit_solution(973416661079791287)
XLA Ops:
  0.7 0.8 broadcast_bitcast_fusion
  1.4 0.7 bitcast_multiply_fusion.2
  2.1 6.0 %collective-permute-start.4 = (f32[2,3,256]{2,1,0:T(4,128)S(1)}, f32[2,3,256]{2,1,0:T(4,128)S(1)}, u32[]{:S(2)}, u32[]{:S(2)}) collective-permute-start(f32[2,3,256]{2,1,0:T(4,128)S(1)} %bitcast_multiply_fusion.2), channel_id=1, source_target_pairs={{2,0},{4,2},{6,4},{8,6},{10,8},{12,10},{14,12},{0,14},{3,1},{5,3},... | collective-permute-start | bytes 18440 | tf_op jit(solution)/shard_map/ppermute | solution.py:19
  8.2 0.7 lt.120
  8.9 0.7 broadcast_in_dim_squeeze.8
  9.6 0.7 copy.384
  11.1 0.8 iota_compare_fusion.4
  11.9 0.8 compare_convert_fusion.1
  12.6 0.7 copy.283
  13.3 0.7 copy.284
  14.1 0.7 pad_bitcast_fusion
  14.8 0.7 reshape_broadcast_in_dim_squeeze.10
  15.6 0.7 reshape_broadcast_in_dim_squeeze.11
  20.0 23.1 %while.55 = (s32[]{:T(128)}, f32[2,3,256]{2,1,0:T(4,128)S(1)}, f32[2,4,3,256]{3,1,2,0:T(4,128)S(1)}, f32[2,3,256]{2,1,0:T(4,128)S(1)}, f32[2,256]{1,0:T(2,128)S(...) while((s32[]{:T(128)}, f32[2,3,256]{2,1,0:T(4,128)S(1)}, ...), condition=%wide.region_14.15_spmd, body=%wide.region_0.14_spmd.sunk | while | flops 19906180 | bytes 14344956 | solution.py:186
  20.2 11.3 %while.58 = (s32[]{:T(128)}, f32[3,256]{1,0:T(4,128)S(1)}, f32[4,3,4,128]{3,2,0,1:T(4,128)S(1)}, f32[1,3,4,128]{3,2,1,0:T(4,128)S(1)}, f32[3,256]{1,0:T(4,128)S(...) while((s32[]{:T(128)}, f32[3,256]{1,0:T(4,128)S(1)}, ...), condition=%wide.region_13.13_spmd, body=%wide.region_1.12_spmd.sunk | while | flops 19906180 | bytes 14031151 | solution.py:174
  21.9 1.0 fusion.153
  22.8 1.0 fusion.154
  23.8 1.0 fusion.155
  24.9 0.6 fusion.156
  27.5 1.0 fusion.153
  28.5 1.0 fusion.154
  29.5 1.0 fusion.155
  30.6 0.6 fusion.156
  31.7 11.3 %while.58 = (s32[]{:T(128)}, f32[3,256]{1,0:T(4,128)S(1)}, f32[4,3,4,128]{3,2,0,1:T(4,128)S(1)}, f32[1,3,4,128]{3,2,1,0:T(4,128)S(1)}, f32[3,256]{1,0:T(4,128)S(...) while((s32[]{:T(128)}, f32[3,256]{1,0:T(4,128)S(1)}, ...), condition=%wide.region_13.13_spmd, body=%wide.region_1.12_spmd.sunk | while | flops 19906180 | bytes 14031151 | solution.py:174
  33.4 1.0 fusion.153
  34.4 1.0 fusion.154
  35.4 1.0 fusion.155
  36.5 0.6 fusion.156
  39.0 1.0 fusion.153
  40.0 1.0 fusion.154
  41.0 1.0 fusion.155
  42.1 0.6 fusion.156
  44.7 1.5 collective-permute-start.11
  46.2 4.8 %collective-permute-done.11 = f32[2,3,256]{2,1,0:T(4,128)S(1)} collective-permute-done((f32[2,3,256]{2,1,0:T(4,128)S(1)}, f32[2,3,256]{2,1,0:T(4,128)S(1)}, u32[]{:S(2)}, u32[]{:S(2)}) %collective-permute-start.11) | collective-permute-done | bytes 6176 | tf_op jit(solution)/shard_map/ppermute | solution.py:19
  51.3 29.5 %psum.14 = f32[8,8]{0,1:T(8,128)S(1)} all-reduce(f32[8,8]{0,1:T(8,128)S(1)} %convolution_bitcast_fusion.1), channel_id=1, replica_groups=mesh['box'=2,'gx'=8,'gy'=2] {'gx','gy'}, use_global_device_ids=true, to_apply=%region_15.16 | all-reduce | flops 64 | bytes 512 | tf_op jit(solution)/shard_map/psum | solution.py:254
  80.9 0.7 cholesky.44
  81.6 0.6 compare_reduce_fusion.1
  82.3 0.6 fusion.88
  82.9 0.7 fusion.107
  83.6 0.7 fusion.106
  130.7 3.5 %collective-permute-done.12 = f32[2,3,256]{2,1,0:T(4,128)S(1)} collective-permute-done((f32[2,3,256]{2,1,0:T(4,128)S(1)}, f32[2,3,256]{2,1,0:T(4,128)S(1)}, u32[]{:S(2)}, u32[]{:S(2)}) %collective-permute-start.12) | collective-permute-done | bytes 6176 | tf_op jit(solution)/shard_map/ppermute | solution.py:19
  135.7 23.1 %while.57 = (s32[]{:T(128)}, f32[2,3,256]{2,1,0:T(4,128)S(1)}, f32[2,4,3,256]{3,1,2,0:T(4,128)S(1)}, f32[2,3,256]{2,1,0:T(4,128)S(1)}, f32[2,256]{1,0:T(2,128)S(...) while((s32[]{:T(128)}, f32[2,3,256]{2,1,0:T(4,128)S(1)}, ...), condition=%wide.region_33.35_spmd, body=%wide.region_19.34_spmd.sunk | while | flops 19906180 | bytes 14344960 | solution.py:186
  135.9 11.3 %while.59 = (s32[]{:T(128)}, f32[3,256]{1,0:T(4,128)S(1)}, f32[4,3,4,128]{3,2,0,1:T(4,128)S(1)}, f32[1,3,4,128]{3,2,1,0:T(4,128)S(1)}, f32[3,256]{1,0:T(4,128)S(...) while((s32[]{:T(128)}, f32[3,256]{1,0:T(4,128)S(1)}, ...), condition=%wide.region_32.33_spmd, body=%wide.region_20.32_spmd.sunk | while | flops 19906180 | bytes 14031151 | solution.py:174
  137.6 1.0 fusion.143
  138.6 1.0 fusion.144
  139.6 1.0 fusion.145
  143.2 1.0 fusion.143
  144.2 1.0 fusion.144
  145.2 1.0 fusion.145
  146.3 0.6 fusion.146
  147.5 11.3 %while.59 = (s32[]{:T(128)}, f32[3,256]{1,0:T(4,128)S(1)}, f32[4,3,4,128]{3,2,0,1:T(4,128)S(1)}, f32[1,3,4,128]{3,2,1,0:T(4,128)S(1)}, f32[3,256]{1,0:T(4,128)S(...) while((s32[]{:T(128)}, f32[3,256]{1,0:T(4,128)S(1)}, ...), condition=%wide.region_32.33_spmd, body=%wide.region_20.32_spmd.sunk | while | flops 19906180 | bytes 14031151 | solution.py:174
  149.2 1.0 fusion.143
  150.2 1.0 fusion.144
  151.2 1.0 fusion.145
  154.8 1.0 fusion.143
  155.8 1.0 fusion.144
  156.8 1.0 fusion.145
  160.7 6.1 %collective-permute-done.19 = f32[2,3,256]{2,1,0:T(4,128)S(1)} collective-permute-done((f32[2,3,256]{2,1,0:T(4,128)S(1)}, f32[2,3,256]{2,1,0:T(4,128)S(1)}, u32[]{:S(2)}, u32[]{:S(2)}) %collective-permute-start.19) | collective-permute-done | bytes 6176 | tf_op jit(solution)/shard_map/ppermute | solution.py:19
  167.1 29.5 %psum.15 = f32[8,8]{0,1:T(8,128)S(1)} all-reduce(f32[8,8]{0,1:T(8,128)S(1)} %convolution_bitcast_fusion), channel_id=1, replica_groups=mesh['box'=2,'gx'=8,'gy'=2] {'gx','gy'}, use_global_device_ids=true, to_apply=%region_34.36 | all-reduce | flops 64 | bytes 512 | tf_op jit(solution)/shard_map/psum | solution.py:254
  196.7 0.7 cholesky.55
  197.4 0.6 compare_reduce_fusion
  198.1 0.6 select_select_fusion
  198.7 0.7 fusion.105
  199.4 0.7 fusion.104
  (432 shorter events, 29.0 us)
Async XLA Ops:
  0.6 19.1 %copy-start.6 = (f32[3]{0:T(128)S(1)}, f32[3]{0:T(128)}, u32[]{:S(2)}) copy-start(f32[3]{0:T(128)} %constant.290.clone) | copy-start | bytes 40
  0.6 18.9 %copy-start.7 = (f32[4,3]{1,0:T(4,128)S(1)}, f32[4,3]{1,0:T(4,128)}, u32[]{:S(2)}) copy-start(f32[4,3]{1,0:T(4,128)} %constant.329) | copy-start | bytes 148
  0.7 19.3 %copy-start = (f32[1,2,256]{2,1,0:T(2,128)S(1)}, f32[1,2,256]{2,1,0:T(2,128)}, u32[]{:S(2)}) copy-start(f32[1,2,256]{2,1,0:T(2,128)} %param.22) | copy-start | bytes 6148
  0.7 19.3 %copy-start.1 = (s32[1,2,256]{2,1,0:T(2,128)S(1)}, s32[1,2,256]{2,1,0:T(2,128)}, u32[]{:S(2)}) copy-start(s32[1,2,256]{2,1,0:T(2,128)} %param.24) | copy-start | bytes 6148
  2.1 14.2 %collective-permute-start.4 = (f32[2,3,256]{2,1,0:T(4,128)S(1)}, f32[2,3,256]{2,1,0:T(4,128)S(1)}, u32[]{:S(2)}, u32[]{:S(2)}) collective-permute-start(f32[2,3,256]{2,1,0:T(4,128)S(1)} %bitcast_multiply_fusion.2), channel_id=1, source_target_pairs={{2,0},{4,2},{6,4},{8,6},{10,8},{12,10},{14,12},{0,14},{3,1},{5,3},... | collective-permute-start | bytes 18440 | tf_op jit(solution)/shard_map/ppermute | solution.py:19
  8.2 8.2 %collective-permute-start.5 = (f32[3,256]{1,0:T(4,128)S(1)}, f32[3,256]{1,0:T(4,128)S(1)}, u32[]{:S(2)}, u32[]{:S(2)}) collective-permute-start(f32[3,256]{1,0:T(4,128)S(1)} %get-tuple-element.1237), channel_id=1, source_target_pairs={{1,0},{0,1},{3,2},{2,3},{5,4},{4,5},{7,6},{6,7},{9,8},{8,9},{11,10... | collective-permute-start | bytes 9224 | tf_op jit(solution)/shard_map/ppermute | solution.py:19
  10.3 7.6 %collective-permute-start = (f32[2,5,256]{2,1,0:T(8,128)S(1)}, f32[2,5,256]{2,1,0:T(8,128)S(1)}, u32[]{:S(2)}, u32[]{:S(2)}) collective-permute-start(f32[2,5,256]{2,1,0:T(8,128)S(1)} %pad_maximum_fusion.4), channel_id=1, source_target_pairs={{2,0},{4,2},{6,4},{8,6},{10,8},{12,10},{14,12},{0,14},{3,1},{5,3},... | collective-permute-start | bytes 30728 | tf_op jit(solution)/shard_map/ppermute | solution.py:19
  10.9 6.1 %collective-permute-start.1 = (f32[5,256]{1,0:T(8,128)S(1)}, f32[5,256]{1,0:T(8,128)S(1)}, u32[]{:S(2)}, u32[]{:S(2)}) collective-permute-start(f32[5,256]{1,0:T(8,128)S(1)} %get-tuple-element.1225), channel_id=1, source_target_pairs={{1,0},{0,1},{3,2},{2,3},{5,4},{4,5},{7,6},{6,7},{9,8},{8,9},{11,10... | collective-permute-start | bytes 15368 | tf_op jit(solution)/shard_map/ppermute | solution.py:19
  16.4 1.2 collective-permute-start.7
  16.7 1.2 collective-permute-start.6
  17.9 1.2 collective-permute-start.3
  18.3 1.2 collective-permute-start.2
  19.9 23.8 %copy-start.3 = (f32[1,2,7,3,256]{4,1,3,2,0:T(2,128)S(1)}, f32[1,2,7,3,256]{4,1,3,2,0:T(2,128)}, u32[]{:S(2)}) copy-start(f32[1,2,7,3,256]{4,1,3,2,0:T(2,128)} %param.28) | copy-start | bytes 129028
  19.9 23.8 %copy-start.4 = (f32[1,2,7,3,256]{4,1,3,2,0:T(2,128)S(1)}, f32[1,2,7,3,256]{4,1,3,2,0:T(2,128)}, u32[]{:S(2)}) copy-start(f32[1,2,7,3,256]{4,1,3,2,0:T(2,128)} %param.27) | copy-start | bytes 129028
  19.9 31.1 %copy-start.2 = (f32[1,2,3,256]{3,1,2,0:T(2,128)S(1)}, f32[1,2,3,256]{3,1,2,0:T(2,128)}, u32[]{:S(2)}) copy-start(f32[1,2,3,256]{3,1,2,0:T(2,128)} %param.26) | copy-start | bytes 18436
  20.0 31.1 %copy-start.5 = (f32[1,2,3,256]{3,1,2,0:T(2,128)S(1)}, f32[1,2,3,256]{3,1,2,0:T(2,128)}, u32[]{:S(2)}) copy-start(f32[1,2,3,256]{3,1,2,0:T(2,128)} %param.25) | copy-start | bytes 18436
  43.1 1.2 collective-permute-start.10
  43.5 1.2 collective-permute-start.9
  43.7 2.5 collective-permute-start.8
  44.7 6.4 %collective-permute-start.11 = (f32[2,3,256]{2,1,0:T(4,128)S(1)}, f32[2,3,256]{2,1,0:T(4,128)S(1)}, u32[]{:S(2)}, u32[]{:S(2)}) collective-permute-start(f32[2,3,256]{2,1,0:T(4,128)S(1)} %fusion.77), channel_id=1, source_target_pairs={{14,0},{0,2},{2,4},{4,6},{6,8},{8,10},{10,12},{12,14},{15,1},{1,3}... | collective-permute-start | bytes 18440 | tf_op jit(solution)/shard_map/ppermute | solution.py:19
  130.4 3.9 %collective-permute-start.12 = (f32[2,3,256]{2,1,0:T(4,128)S(1)}, f32[2,3,256]{2,1,0:T(4,128)S(1)}, u32[]{:S(2)}, u32[]{:S(2)}) collective-permute-start(f32[2,3,256]{2,1,0:T(4,128)S(1)} %fusion.59), channel_id=1, source_target_pairs={{2,0},{4,2},{6,4},{8,6},{10,8},{12,10},{14,12},{0,14},{3,1},{5,3},... | collective-permute-start | bytes 18440 | tf_op jit(solution)/shard_map/ppermute | solution.py:19
  130.7 4.2 %collective-permute-start.13 = (f32[3,256]{1,0:T(4,128)S(1)}, f32[3,256]{1,0:T(4,128)S(1)}, u32[]{:S(2)}, u32[]{:S(2)}) collective-permute-start(f32[3,256]{1,0:T(4,128)S(1)} %get-tuple-element.1231), channel_id=1, source_target_pairs={{1,0},{0,1},{3,2},{2,3},{5,4},{4,5},{7,6},{6,7},{9,8},{8,9},{11,10... | collective-permute-start | bytes 9224 | tf_op jit(solution)/shard_map/ppermute | solution.py:19
  134.3 1.2 collective-permute-start.15
  134.3 1.3 collective-permute-start.14
  158.9 1.2 collective-permute-start.18
  159.3 1.2 collective-permute-start.17
  159.5 1.2 collective-permute-start.16
  160.5 6.4 %collective-permute-start.19 = (f32[2,3,256]{2,1,0:T(4,128)S(1)}, f32[2,3,256]{2,1,0:T(4,128)S(1)}, u32[]{:S(2)}, u32[]{:S(2)}) collective-permute-start(f32[2,3,256]{2,1,0:T(4,128)S(1)} %fusion.75), channel_id=1, source_target_pairs={{14,0},{0,2},{2,4},{4,6},{6,8},{8,10},{10,12},{12,14},{15,1},{1,3}... | collective-permute-start | bytes 18440 | tf_op jit(solution)/shard_map/ppermute | solution.py:19
  246.1 0.7 copy-start.8
where the time goes:
time: 249 us; the launch traced here: 247 us
  between operations  92.8 us (37%)
  blocking collectives  59 us (24%)
  other arithmetic  47 us (19%)
  waiting for transfers between devices  18.3 us (7%)
  local copies, waits for them, and re-layouts  15.3 us (6%)
  starting transfers between devices  12.4 us (5%)
    psum x2, blocking collectives, body(): gram_matrix = lax.psum(local_gram, ('gx', 'gy'))  59 us
    ppermute x20, waiting for transfers between devices, from_behind(): return lax.ppermute(block, axis, route)  18.3 us
    ppermute x20, starting transfers between devices, from_behind(): return lax.ppermute(block, axis, route)  12.4 us
    div x16, other arithmetic, pair_terms(): isotropic = weight * -jnp.expm1(-damped) / cube_dist  10.8 us
    reduce_sum x8, other arithmetic, field_sources(): projected = jnp.sum(displace * target_dipole[:, :, None], axis=0)  8.01 us
    mul x8, other arithmetic, field_targets(): tensorial * projected  7.77 us
    reduce_sum x8, other arithmetic, field_sources(): jnp.sum(displace * (tensorial * projected)[None], axis=1)  5.08 us
  transfers between devices with their start and end apart: 20, of which 14 were waited for; matrix products, arithmetic and copies ran while one was open for 3% of the time, Pallas kernels for 0%

commit v1 on v0

--- a/solution.py
+++ b/solution.py
@@ -251,7 +251,8 @@
             precision=lax.Precision.HIGHEST,
             preferred_element_type=jnp.float32,
         )
-        gram_matrix = lax.psum(local_gram, ("gx", "gy"))
+        found_now = lax.all_gather(local_gram, ("gx", "gy"))
+        gram_matrix = jnp.sum(found_now, axis=0)
         weights = diis_weights(gram_matrix)
         current = jnp.sum(weights[:, None, None, None] * outputs_all, axis=0)
         stored_out = outputs_all[1:]

time: 249 us -> 226 us (0.908)
  blocking collectives: 59 us -> 36.6 us
  waiting for transfers between devices: 18.3 us -> 13.4 us
  starting transfers between devices: 12.4 us -> 17.2 us
    psum x2 -> x0, blocking collectives: 59 us -> none  [body(): gram_matrix = lax.psum(local_gram, ('gx', 'gy'))]
    all_gather x0 -> x2, blocking collectives: none -> 36.6 us  [body(): found_now = lax.all_gather(local_gram, ('gx', 'gy'))]
    ppermute x20, starting transfers between devices: 12.4 us -> 17.2 us  [from_behind(): return lax.ppermute(block, axis, route)]
    ppermute x20, waiting for transfers between devices: 18.3 us -> 13.4 us  [from_behind(): return lax.ppermute(block, axis, route)]
  transfers between devices with their start and end apart: 20 -> 20, of which waited for: 14 -> 13; matrix products, arithmetic and copies ran while one was open for 3% -> 3% of each run, Pallas kernels for 0% -> 0%
where the time goes in v1:
time: 226 us; the launch traced here: 224 us
  between operations  92.8 us (41%)
  other arithmetic  47.1 us (21%)
  blocking collectives  36.6 us (16%)
  starting transfers between devices  17.2 us (8%)
  local copies, waits for them, and re-layouts  15.3 us (7%)
  waiting for transfers between devices  13.4 us (6%)
    all_gather x2, blocking collectives, body(): found_now = lax.all_gather(local_gram, ('gx', 'gy'))  36.6 us
    ppermute x20, starting transfers between devices, from_behind(): return lax.ppermute(block, axis, route)  17.2 us
    ppermute x20, waiting for transfers between devices, from_behind(): return lax.ppermute(block, axis, route)  13.4 us
    div x16, other arithmetic, pair_terms(): isotropic = weight * -jnp.expm1(-damped) / cube_dist  10.8 us
    reduce_sum x8, other arithmetic, field_sources(): projected = jnp.sum(displace * target_dipole[:, :, None], axis=0)  8.01 us
    mul x8, other arithmetic, field_targets(): tensorial * projected  7.77 us
    reduce_sum x8, other arithmetic, field_sources(): jnp.sum(displace * (tensorial * projected)[None], axis=1)  5.08 us
  transfers between devices with their start and end apart: 20, of which 13 were waited for; matrix products, arithmetic and copies ran while one was open for 3% of the time, Pallas kernels for 0%

profile of v1, /device:TPU:0, one launch (start us, length us, event | category | flops | bytes accessed | tf_op | source)
XLA Modules:
  0.0 224.4 jit_solution(10350353775158289384)
XLA Ops:
  0.7 0.8 broadcast_bitcast_fusion
  1.4 0.7 bitcast_multiply_fusion.2
  2.1 6.0 %collective-permute-start.4 = (f32[2,3,256]{2,1,0:T(4,128)S(1)}, f32[2,3,256]{2,1,0:T(4,128)S(1)}, u32[]{:S(2)}, u32[]{:S(2)}) collective-permute-start(f32[2,3,256]{2,1,0:T(4,128)S(1)} %bitcast_multiply_fusion.2), channel_id=1, source_target_pairs={{2,0},{4,2},{6,4},{8,6},{10,8},{12,10},{14,12},{0,14},{3,1},{5,3},... | collective-permute-start | bytes 18440 | tf_op jit(solution)/shard_map/ppermute | solution.py:19
  8.2 0.7 lt.120
  8.9 0.7 broadcast_in_dim_squeeze.8
  9.6 0.7 copy.368
  11.1 0.8 iota_compare_fusion.4
  11.9 0.8 compare_convert_fusion.1
  12.6 0.7 copy.271
  13.3 0.7 copy.272
  14.1 0.7 pad_bitcast_fusion
  14.8 0.7 reshape_broadcast_in_dim_squeeze.10
  15.6 0.7 reshape_broadcast_in_dim_squeeze.11
  20.0 23.1 %while.55 = (s32[]{:T(128)}, f32[2,3,256]{2,1,0:T(4,128)S(1)}, f32[2,4,3,256]{3,1,2,0:T(4,128)S(1)}, f32[2,3,256]{2,1,0:T(4,128)S(1)}, f32[2,256]{1,0:T(2,128)S(...) while((s32[]{:T(128)}, f32[2,3,256]{2,1,0:T(4,128)S(1)}, ...), condition=%wide.region_14.15_spmd, body=%wide.region_0.14_spmd.sunk | while | flops 19906180 | bytes 14344956 | solution.py:186
  20.2 11.3 %while.58 = (s32[]{:T(128)}, f32[3,256]{1,0:T(4,128)S(1)}, f32[4,3,4,128]{3,2,0,1:T(4,128)S(1)}, f32[1,3,4,128]{3,2,1,0:T(4,128)S(1)}, f32[3,256]{1,0:T(4,128)S(...) while((s32[]{:T(128)}, f32[3,256]{1,0:T(4,128)S(1)}, ...), condition=%wide.region_13.13_spmd, body=%wide.region_1.12_spmd.sunk | while | flops 19906180 | bytes 14031151 | solution.py:174
  21.9 1.0 fusion.153
  22.8 1.0 fusion.154
  23.8 1.0 fusion.155
  24.9 0.6 fusion.156
  27.5 1.0 fusion.153
  28.5 1.0 fusion.154
  29.5 1.0 fusion.155
  30.6 0.6 fusion.156
  31.7 11.3 %while.58 = (s32[]{:T(128)}, f32[3,256]{1,0:T(4,128)S(1)}, f32[4,3,4,128]{3,2,0,1:T(4,128)S(1)}, f32[1,3,4,128]{3,2,1,0:T(4,128)S(1)}, f32[3,256]{1,0:T(4,128)S(...) while((s32[]{:T(128)}, f32[3,256]{1,0:T(4,128)S(1)}, ...), condition=%wide.region_13.13_spmd, body=%wide.region_1.12_spmd.sunk | while | flops 19906180 | bytes 14031151 | solution.py:174
  33.4 1.0 fusion.153
  34.4 1.0 fusion.154
  35.4 1.0 fusion.155
  36.5 0.6 fusion.156
  39.0 1.0 fusion.153
  40.0 1.0 fusion.154
  41.0 1.0 fusion.155
  44.7 1.5 collective-permute-start.11
  46.2 4.8 %collective-permute-done.11 = f32[2,3,256]{2,1,0:T(4,128)S(1)} collective-permute-done((f32[2,3,256]{2,1,0:T(4,128)S(1)}, f32[2,3,256]{2,1,0:T(4,128)S(1)}, u32[]{:S(2)}, u32[]{:S(2)}) %collective-permute-start.11) | collective-permute-done | bytes 6176 | tf_op jit(solution)/shard_map/ppermute | solution.py:19
  51.3 17.3 %all-gather = f32[128,8]{1,0:T(8,128)S(1)} all-gather(f32[8,8]{1,0:T(8,128)S(1)} %convolution_bitcast_fusion.1), channel_id=2, replica_groups=mesh['box'=2,'gx'=8,'gy'=2] {'gx','gy'}, dimensions={0}, use_global_device_ids=true | all-gather | bytes 4352 | tf_op jit(solution)/shard_map/all_gather | solution.py:254
  68.7 0.7 cholesky.44
  69.4 0.6 compare_reduce_fusion.1
  70.1 0.6 fusion.88
  70.7 0.7 fusion.107
  71.4 0.7 fusion.106
  118.2 2.2 collective-permute-start.12
  120.5 1.6 collective-permute-done.12
  123.5 23.1 %while.57 = (s32[]{:T(128)}, f32[2,3,256]{2,1,0:T(4,128)S(1)}, f32[2,4,3,256]{3,1,2,0:T(4,128)S(1)}, f32[2,3,256]{2,1,0:T(4,128)S(1)}, f32[2,256]{1,0:T(2,128)S(...) while((s32[]{:T(128)}, f32[2,3,256]{2,1,0:T(4,128)S(1)}, ...), condition=%wide.region_33.35_spmd, body=%wide.region_19.34_spmd.sunk | while | flops 19906180 | bytes 14344960 | solution.py:186
  123.8 11.3 %while.59 = (s32[]{:T(128)}, f32[3,256]{1,0:T(4,128)S(1)}, f32[4,3,4,128]{3,2,0,1:T(4,128)S(1)}, f32[1,3,4,128]{3,2,1,0:T(4,128)S(1)}, f32[3,256]{1,0:T(4,128)S(...) while((s32[]{:T(128)}, f32[3,256]{1,0:T(4,128)S(1)}, ...), condition=%wide.region_32.33_spmd, body=%wide.region_20.32_spmd.sunk | while | flops 19906180 | bytes 14031151 | solution.py:174
  125.4 1.0 fusion.143
  126.4 1.0 fusion.144
  127.4 1.0 fusion.145
  131.1 1.0 fusion.143
  132.1 1.0 fusion.144
  133.1 1.0 fusion.145
  135.3 11.3 %while.59 = (s32[]{:T(128)}, f32[3,256]{1,0:T(4,128)S(1)}, f32[4,3,4,128]{3,2,0,1:T(4,128)S(1)}, f32[1,3,4,128]{3,2,1,0:T(4,128)S(1)}, f32[3,256]{1,0:T(4,128)S(...) while((s32[]{:T(128)}, f32[3,256]{1,0:T(4,128)S(1)}, ...), condition=%wide.region_32.33_spmd, body=%wide.region_20.32_spmd.sunk | while | flops 19906180 | bytes 14031151 | solution.py:174
  137.0 1.0 fusion.143
  138.0 1.0 fusion.144
  139.0 1.0 fusion.145
  142.6 1.0 fusion.143
  143.6 1.0 fusion.144
  144.6 1.0 fusion.145
  148.3 2.9 %collective-permute-start.19 = (f32[2,3,256]{2,1,0:T(4,128)S(1)}, f32[2,3,256]{2,1,0:T(4,128)S(1)}, u32[]{:S(2)}, u32[]{:S(2)}) collective-permute-start(f32[2,3,256]{2,1,0:T(4,128)S(1)} %fusion.75), channel_id=1, source_target_pairs={{14,0},{0,2},{2,4},{4,6},{6,8},{8,10},{10,12},{12,14},{15,1},{1,3}... | collective-permute-start | bytes 18440 | tf_op jit(solution)/shard_map/ppermute | solution.py:19
  151.3 3.4 %collective-permute-done.19 = f32[2,3,256]{2,1,0:T(4,128)S(1)} collective-permute-done((f32[2,3,256]{2,1,0:T(4,128)S(1)}, f32[2,3,256]{2,1,0:T(4,128)S(1)}, u32[]{:S(2)}, u32[]{:S(2)}) %collective-permute-start.19) | collective-permute-done | bytes 6176 | tf_op jit(solution)/shard_map/ppermute | solution.py:19
  154.9 19.3 %all-gather.1 = f32[128,8]{1,0:T(8,128)S(1)} all-gather(f32[8,8]{1,0:T(8,128)S(1)} %convolution_bitcast_fusion), channel_id=3, replica_groups=mesh['box'=2,'gx'=8,'gy'=2] {'gx','gy'}, dimensions={0}, use_global_device_ids=true | all-gather | bytes 4352 | tf_op jit(solution)/shard_map/all_gather | solution.py:254
  174.3 0.7 cholesky.55
  175.0 0.6 compare_reduce_fusion
  175.7 0.6 select_select_fusion
  176.3 0.7 fusion.105
  177.0 0.7 fusion.104
  (434 shorter events, 29.8 us)
Async XLA Ops:
  0.6 19.1 %copy-start.6 = (f32[3]{0:T(128)S(1)}, f32[3]{0:T(128)}, u32[]{:S(2)}) copy-start(f32[3]{0:T(128)} %constant.290.clone) | copy-start | bytes 40
  0.6 18.9 %copy-start.7 = (f32[4,3]{1,0:T(4,128)S(1)}, f32[4,3]{1,0:T(4,128)}, u32[]{:S(2)}) copy-start(f32[4,3]{1,0:T(4,128)} %constant.329) | copy-start | bytes 148
  0.7 19.3 %copy-start = (f32[1,2,256]{2,1,0:T(2,128)S(1)}, f32[1,2,256]{2,1,0:T(2,128)}, u32[]{:S(2)}) copy-start(f32[1,2,256]{2,1,0:T(2,128)} %param.22) | copy-start | bytes 6148
  0.7 19.3 %copy-start.1 = (s32[1,2,256]{2,1,0:T(2,128)S(1)}, s32[1,2,256]{2,1,0:T(2,128)}, u32[]{:S(2)}) copy-start(s32[1,2,256]{2,1,0:T(2,128)} %param.24) | copy-start | bytes 6148
  2.1 14.2 %collective-permute-start.4 = (f32[2,3,256]{2,1,0:T(4,128)S(1)}, f32[2,3,256]{2,1,0:T(4,128)S(1)}, u32[]{:S(2)}, u32[]{:S(2)}) collective-permute-start(f32[2,3,256]{2,1,0:T(4,128)S(1)} %bitcast_multiply_fusion.2), channel_id=1, source_target_pairs={{2,0},{4,2},{6,4},{8,6},{10,8},{12,10},{14,12},{0,14},{3,1},{5,3},... | collective-permute-start | bytes 18440 | tf_op jit(solution)/shard_map/ppermute | solution.py:19
  8.2 8.2 %collective-permute-start.5 = (f32[3,256]{1,0:T(4,128)S(1)}, f32[3,256]{1,0:T(4,128)S(1)}, u32[]{:S(2)}, u32[]{:S(2)}) collective-permute-start(f32[3,256]{1,0:T(4,128)S(1)} %get-tuple-element.1237), channel_id=1, source_target_pairs={{1,0},{0,1},{3,2},{2,3},{5,4},{4,5},{7,6},{6,7},{9,8},{8,9},{11,10... | collective-permute-start | bytes 9224 | tf_op jit(solution)/shard_map/ppermute | solution.py:19
  10.3 7.6 %collective-permute-start = (f32[2,5,256]{2,1,0:T(8,128)S(1)}, f32[2,5,256]{2,1,0:T(8,128)S(1)}, u32[]{:S(2)}, u32[]{:S(2)}) collective-permute-start(f32[2,5,256]{2,1,0:T(8,128)S(1)} %pad_maximum_fusion.4), channel_id=1, source_target_pairs={{2,0},{4,2},{6,4},{8,6},{10,8},{12,10},{14,12},{0,14},{3,1},{5,3},... | collective-permute-start | bytes 30728 | tf_op jit(solution)/shard_map/ppermute | solution.py:19
  10.9 6.1 %collective-permute-start.1 = (f32[5,256]{1,0:T(8,128)S(1)}, f32[5,256]{1,0:T(8,128)S(1)}, u32[]{:S(2)}, u32[]{:S(2)}) collective-permute-start(f32[5,256]{1,0:T(8,128)S(1)} %get-tuple-element.1225), channel_id=1, source_target_pairs={{1,0},{0,1},{3,2},{2,3},{5,4},{4,5},{7,6},{6,7},{9,8},{8,9},{11,10... | collective-permute-start | bytes 15368 | tf_op jit(solution)/shard_map/ppermute | solution.py:19
  16.4 1.2 collective-permute-start.7
  16.7 1.2 collective-permute-start.6
  17.9 1.2 collective-permute-start.3
  18.3 1.2 collective-permute-start.2
  19.9 23.8 %copy-start.3 = (f32[1,2,7,3,256]{4,1,3,2,0:T(2,128)S(1)}, f32[1,2,7,3,256]{4,1,3,2,0:T(2,128)}, u32[]{:S(2)}) copy-start(f32[1,2,7,3,256]{4,1,3,2,0:T(2,128)} %param.28) | copy-start | bytes 129028
  19.9 23.8 %copy-start.4 = (f32[1,2,7,3,256]{4,1,3,2,0:T(2,128)S(1)}, f32[1,2,7,3,256]{4,1,3,2,0:T(2,128)}, u32[]{:S(2)}) copy-start(f32[1,2,7,3,256]{4,1,3,2,0:T(2,128)} %param.27) | copy-start | bytes 129028
  19.9 31.1 %copy-start.2 = (f32[1,2,3,256]{3,1,2,0:T(2,128)S(1)}, f32[1,2,3,256]{3,1,2,0:T(2,128)}, u32[]{:S(2)}) copy-start(f32[1,2,3,256]{3,1,2,0:T(2,128)} %param.26) | copy-start | bytes 18436
  20.0 31.1 %copy-start.5 = (f32[1,2,3,256]{3,1,2,0:T(2,128)S(1)}, f32[1,2,3,256]{3,1,2,0:T(2,128)}, u32[]{:S(2)}) copy-start(f32[1,2,3,256]{3,1,2,0:T(2,128)} %param.25) | copy-start | bytes 18436
  43.1 1.2 collective-permute-start.10
  43.5 1.2 collective-permute-start.9
  43.7 2.5 %collective-permute-start.8 = (f32[3,256]{1,0:T(4,128)S(1)}, f32[3,256]{1,0:T(4,128)S(1)}, u32[]{:S(2)}, u32[]{:S(2)}) collective-permute-start(f32[3,256]{1,0:T(4,128)S(1)} %get-tuple-element.1218), channel_id=1, source_target_pairs={{1,0},{0,1},{3,2},{2,3},{5,4},{4,5},{7,6},{6,7},{9,8},{8,9},{11,10... | collective-permute-start | bytes 9224 | tf_op jit(solution)/shard_map/ppermute | solution.py:19
  44.7 6.4 %collective-permute-start.11 = (f32[2,3,256]{2,1,0:T(4,128)S(1)}, f32[2,3,256]{2,1,0:T(4,128)S(1)}, u32[]{:S(2)}, u32[]{:S(2)}) collective-permute-start(f32[2,3,256]{2,1,0:T(4,128)S(1)} %fusion.77), channel_id=1, source_target_pairs={{14,0},{0,2},{2,4},{4,6},{6,8},{8,10},{10,12},{12,14},{15,1},{1,3}... | collective-permute-start | bytes 18440 | tf_op jit(solution)/shard_map/ppermute | solution.py:19
  118.2 3.9 %collective-permute-start.12 = (f32[2,3,256]{2,1,0:T(4,128)S(1)}, f32[2,3,256]{2,1,0:T(4,128)S(1)}, u32[]{:S(2)}, u32[]{:S(2)}) collective-permute-start(f32[2,3,256]{2,1,0:T(4,128)S(1)} %fusion.59), channel_id=1, source_target_pairs={{2,0},{4,2},{6,4},{8,6},{10,8},{12,10},{14,12},{0,14},{3,1},{5,3},... | collective-permute-start | bytes 18440 | tf_op jit(solution)/shard_map/ppermute | solution.py:19
  120.5 2.2 collective-permute-start.13
  122.1 1.2 collective-permute-start.15
  122.1 1.3 collective-permute-start.14
  146.7 1.2 collective-permute-start.18
  147.1 1.2 collective-permute-start.17
  147.3 3.9 %collective-permute-start.16 = (f32[3,256]{1,0:T(4,128)S(1)}, f32[3,256]{1,0:T(4,128)S(1)}, u32[]{:S(2)}, u32[]{:S(2)}) collective-permute-start(f32[3,256]{1,0:T(4,128)S(1)} %get-tuple-element.1213), channel_id=1, source_target_pairs={{1,0},{0,1},{3,2},{2,3},{5,4},{4,5},{7,6},{6,7},{9,8},{8,9},{11,10... | collective-permute-start | bytes 9224 | tf_op jit(solution)/shard_map/ppermute | solution.py:19
  148.3 6.4 %collective-permute-start.19 = (f32[2,3,256]{2,1,0:T(4,128)S(1)}, f32[2,3,256]{2,1,0:T(4,128)S(1)}, u32[]{:S(2)}, u32[]{:S(2)}) collective-permute-start(f32[2,3,256]{2,1,0:T(4,128)S(1)} %fusion.75), channel_id=1, source_target_pairs={{14,0},{0,2},{2,4},{4,6},{6,8},{8,10},{10,12},{12,14},{15,1},{1,3}... | collective-permute-start | bytes 18440 | tf_op jit(solution)/shard_map/ppermute | solution.py:19
  223.7 0.7 copy-start.8
